TPU v7x, 32 devices: a whole 2x2x4 slice. The times are simulated.
32 devices in a mesh: dp: 4 (over y, x), ctx: 8 (over z, core).
Axes of the slice: x: 2, y: 2, z: 4, core: 2. Of those that a mesh axis runs over, the one named last changes fastest.
Arguments:
- inputs: bfloat16 [4, 2048, 4096], P('dp', 'ctx'), may hold values from -6 to 6
- query_weight: bfloat16 [4096, 128], P('dp'), may hold values from -0.09375 to 0.09375
- key_weight: bfloat16 [4096, 128], P('dp'), may hold values from -0.09375 to 0.09375
- value_weight: bfloat16 [4096, 2048], P('dp'), may hold values from -0.09375 to 0.09375
- lambda_weight: bfloat16 [4096, 320], P('dp'), may hold values from -0.09375 to 0.09375
- log_decay: float32 [4, 2048, 16], P('dp', 'ctx'), may hold values from -1 to 0, as said below
- norm_gain: float32 [2048], replicated, may hold values from 0.5 to 1.5
Outputs:
- outputs: bfloat16 [4, 2048, 2048], P('dp', 'ctx')
Inputs may be any that keep to these rules, and one draw needn't show every extreme that they name: `log_decay`: entries are not positive.
All inputs are finite; a program needn't handle non-finite values.
Results may differ from a plain program's by a relative error of at most 0.0072.
Values may be sent and summed in bfloat16 or wider, within the bound.
A program may use at most 128 MiB of HBM per device.

v0:
```python
import math

import jax
import jax.numpy as jnp
from jax import lax
from jax.sharding import PartitionSpec as P

HIGHEST = lax.Precision.HIGHEST


def from_partner(block, axis, stride):
    count = lax.axis_size(axis)
    route = []
    for low in range(count):
        high = low | 1 << stride
        if high != low and high < count:
            route += [(low, high), (high, low)]
    return lax.ppermute(block, axis, route)


def level_masks(length):
    depth = length.bit_length() - 1
    token_place = jnp.arange(length, dtype=jnp.int32)
    differ = jnp.bitwise_xor(token_place[:, None], token_place[None, :])
    level = jnp.zeros((length, length), jnp.int32)
    for power in range(depth):
        level = level + (differ >= 1 << power).astype(jnp.int32)
    levels = jnp.arange(depth + 1, dtype=jnp.int32)
    return (level[None, :, :] == levels[:, None, None]).astype(jnp.float32)


def block_terms(query_rows, key_rows, value_rows, lambdas, log_decay, masks):
    length, heads = log_decay.shape
    state_dim = query_rows.shape[1]
    head_dim = value_rows.shape[1] // heads
    inner = masks.shape[0]
    weights_all = lambdas.reshape(length, heads, -1)
    cumulative = jnp.cumsum(log_decay, axis=0)
    scores = lax.dot_general(
        query_rows, key_rows, (((1,), (1,)), ((), ())), preferred_element_type=jnp.float32
    ) / math.sqrt(state_dim)
    level_weight = jnp.einsum("lts,thl->hts", masks, weights_all[:, :, :inner], precision=HIGHEST)
    token_place = jnp.arange(length, dtype=jnp.int32)
    causal = token_place[:, None] >= token_place[None, :]
    spread = jnp.transpose(cumulative)
    distance = spread[:, :, None] - spread[:, None, :]
    decay = jnp.exp(jnp.where(causal[None], distance, -jnp.inf))
    mix = (level_weight * decay * scores[None]).astype(jnp.bfloat16)
    values = value_rows.reshape(length, heads, head_dim)
    near = jnp.einsum("hts,shd->thd", mix, values, preferred_element_type=jnp.float32)
    remain = jnp.exp(cumulative[-1][None, :] - cumulative)
    keyed = (key_rows.astype(jnp.float32)[:, None, :] * remain[:, :, None]).astype(jnp.bfloat16)
    state = jnp.einsum("chs,chd->hsd", keyed, values, preferred_element_type=jnp.float32)
    total = jnp.exp(cumulative[-1])
    return (near, state, total, cumulative, weights_all)


def finish(mixed, norm_gain):
    heads = mixed.shape[-2]
    mean_square = jnp.mean(mixed * mixed, axis=-1, keepdims=True)
    return (mixed * lax.rsqrt(mean_square + 1e-05) * norm_gain.reshape(heads, -1)).astype(
        jnp.bfloat16
    )


def make_fold(tokens):

    def accumulate(totals, pieces, start):
        return tuple(
            (jnp.dot(tokens, piece, preferred_element_type=jnp.float32) for piece in pieces)
        )

    return accumulate


def zeros_for(length, weights):
    return tuple((jnp.zeros((length, weight.shape[1]), jnp.float32) for weight in weights))


def per_device(inputs, query_weight, key_weight, value_weight, lambda_weight, log_decay, norm_gain):
    tokens = inputs[0]
    decays = log_decay[0]
    length = tokens.shape[0]
    accumulate = make_fold(tokens)
    query_sum, key_sum, value_sum, lambda_sum = accumulate(
        zeros_for(length, (query_weight, key_weight, value_weight, lambda_weight)),
        (
            lax.all_gather(query_weight, "dp", axis=0, tiled=True),
            lax.all_gather(key_weight, "dp", axis=0, tiled=True),
            lax.all_gather(value_weight, "dp", axis=0, tiled=True),
            lax.all_gather(lambda_weight, "dp", axis=0, tiled=True),
        ),
        jnp.int32(0),
    )
    query_rows = query_sum.astype(jnp.bfloat16)
    key_rows = key_sum.astype(jnp.bfloat16)
    value_rows = value_sum.astype(jnp.bfloat16)
    lambdas = jax.nn.softplus(lambda_sum)
    masks = level_masks(length)
    inner = masks.shape[0]
    scale = 1.0 / math.sqrt(query_rows.shape[1])
    near, state, total, cumulative, weights_all = block_terms(
        query_rows, key_rows, value_rows, lambdas, decays, masks
    )
    index = lax.axis_index("ctx")
    bits = lax.axis_size("ctx").bit_length() - 1
    block_state = state
    block_total = total
    carry_decay = jnp.ones_like(total)
    growth = jnp.exp(cumulative)
    mixed = near
    for level_bit in range(bits):
        other_state, other_total = from_partner((block_state, block_total), "ctx", level_bit)
        upper = (index >> level_bit & 1).astype(jnp.float32)
        carried = (carry_decay[:, None, None] * other_state).astype(jnp.bfloat16)
        reach = jnp.einsum("ts,hsd->thd", query_rows, carried, preferred_element_type=jnp.float32)
        factor = weights_all[:, :, inner + level_bit] * growth * (scale * upper)
        mixed = mixed + factor[..., None] * reach
        if level_bit + 1 < bits:
            block_state = jnp.where(
                upper > 0,
                block_total[:, None, None] * other_state + block_state,
                other_total[:, None, None] * block_state + other_state,
            )
            carry_decay = jnp.where(upper > 0, other_total * carry_decay, carry_decay)
            block_total = block_total * other_total
    return finish(mixed, norm_gain).reshape(1, length, -1)


def solution(mesh):
    return jax.shard_map(
        per_device,
        mesh=mesh,
        in_specs=(
            P("dp", "ctx", None),
            P("dp", None),
            P("dp", None),
            P("dp", None),
            P("dp", None),
            P("dp", "ctx", None),
            P(),
        ),
        out_specs=P("dp", "ctx", None),
        check_vma=False,
    )
```

profile of v0, /device:TPU:0, one launch (start us, length us, event | category | flops | bytes accessed | tf_op | source)
XLA Modules:
  0.0 352.5 jit_solution(18058356890450895991)
XLA Ops:
  9.9 28.5 %all-gather.11.cloned.1.call-done = bf16[4096,128]{1,0:T(8,128)(2,1)} async-done(((bf16[1024,128]{1,0:T(8,128)(2,1)}), bf16[4096,128]{1,0:T(8,128)(2,1)}) %all-gather.11.cloned.1.call-update) | async-done | bytes 1048592 | tf_op jit(solution)/shard_map/all_gather | solution.py:89
  38.4 1.9 fusion.21
  40.5 39.3 %all-gather.7.cloned.1.call-done = bf16[4096,320]{0,1:T(8,128)(2,1)} async-done(((bf16[1024,320]{0,1:T(8,128)(2,1)}), bf16[4096,320]{0,1:T(8,128)(2,1)}) %all-gather.7.cloned.1.call-update) | async-done | bytes 2621456 | tf_op jit(solution)/shard_map/all_gather | solution.py:91
  79.8 2.7 compare_select_fusion
  83.4 155.6 %all-gather.5.cloned.1.call-done = bf16[4096,2048]{1,0:T(8,128)(2,1)} async-done(((bf16[1024,2048]{1,0:T(8,128)(2,1)}), bf16[4096,2048]{1,0:T(8,128)(2,1)}) %all-gather.5.cloned.1.call-update) | async-done | bytes 16777232 | tf_op jit(solution)/shard_map/all_gather | solution.py:90
  239.0 8.3 %fusion.15 = bf16[32,16,8,128]{3,2,1,0:T(8,128)(2,1)S(1)} fusion(bf16[4096,2048]{1,0:T(8,128)(2,1)} %all-gather.5.cloned.1.call-done, bf16[1,256,4096]{2,1,0:T(8,128)(2,1)S(1)} %copy-done), kind=kOutput, calls=%fused_computation.22 | convolution fusion | flops 4295491584 | bytes 19922944 | tf_op jit(solution)/shard_map/dot_general | solution.py:70
  250.2 1.4 collective-permute-done.1
  251.5 3.0 fusion.48
  254.6 1.5 collective-permute-start.2
  258.0 21.9 %collective-permute-done.3 = f32[16]{0:T(128)S(1)} collective-permute-done((f32[16]{0:T(128)S(1)}, f32[16]{0:T(128)S(1)}, u32[]{:S(2)}, u32[]{:S(2)}) %collective-permute-start.3) | collective-permute-done | bytes 96 | tf_op jit(solution)/shard_map/ppermute | solution.py:18
  280.5 1.9 fusion.18
  283.3 2.5 copy.51
  285.9 2.9 multiply_convert_fusion.4
  288.8 2.4 collective-permute-start.4
  291.3 3.6 %fusion.1 = bf16[16,256,256]{2,0,1:T(8,128)(2,1)S(1)} fusion(f32[256,16,9]{2,1,0:T(8,128)S(1)} %copy-done.3, f32[256,256]{1,0:T(8,128)S(1)} %copy-done.9, f32[16,256]{1,0:T(8,128)S(1)} %copy-done.15, f32[16,256]{0,1:T(8,128)S(1)} %copy-done.11, s32[256,256]{1,0:T(8,128)S(1)} %copy-done.10, pred[256,256]{1,0:T(8,128)(4,1)S(1)} %copy-done.16), kind=kOutput, calls=%fused_computation.2 | convolution fusion | flops 119078912 | bytes 2867200 | tf_op jit(solution)/shard_map/lts,thl->hts/dot_general | solution.py:42
  294.9 2.3 fusion.12
  297.2 1.0 copy.45
  298.2 2.8 fusion.50
  301.3 1.8 fusion.51
  303.1 34.4 %collective-permute-done.4 = f32[16,128,128]{2,1,0:T(8,128)} collective-permute-done((f32[16,128,128]{2,1,0:T(8,128)}, f32[16,128,128]{2,1,0:T(8,128)}, u32[]{:S(2)}, u32[]{:S(2)}) %collective-permute-start.4) | collective-permute-done | bytes 1048608 | tf_op jit(solution)/shard_map/ppermute | solution.py:18
  337.5 1.4 multiply_convert_fusion.3
  339.7 1.1 copy-done.1
  340.8 3.3 multiply_reduce_fusion
  344.5 1.4 copy.49
  (91 shorter events, 11.9 us)
Async XLA Ops:
  6.5 31.9 %copy-start = (bf16[1,256,4096]{2,1,0:T(8,128)(2,1)S(1)}, bf16[1,256,4096]{2,1,0:T(8,128)(2,1)}, u32[]{:S(2)}) copy-start(bf16[1,256,4096]{2,1,0:T(8,128)(2,1)} %param.7) | copy-start | bytes 6291460
  6.5 31.9 %all-gather.11.cloned.1.call-start = ((), (), s32[]{:S(2)}) async-start(), calls=%async_computation.3 | async-start | bytes 1310720 | tf_op jit(solution)/shard_map/all_gather | solution.py:89
  7.3 72.6 %all-gather.7.cloned.1.call-start = ((), (), s32[]{:S(2)}) async-start(), calls=%async_computation.1 | async-start | bytes 3276800 | tf_op jit(solution)/shard_map/all_gather | solution.py:91
  8.0 231.0 %all-gather.5.cloned.1.call-start = ((), (), s32[]{:S(2)}) async-start(), calls=%async_computation | async-start | bytes 20971520 | tf_op jit(solution)/shard_map/all_gather | solution.py:90
  8.8 271.7 %all-gather.9.cloned.1.call-start = ((), (), s32[]{:S(2)}) async-start(), calls=%async_computation.2 | async-start | bytes 1310720 | tf_op jit(solution)/shard_map/all_gather | solution.py:88
  9.7 247.6 %copy-start.14 = (f32[16,256]{1,0:T(8,128)}, f32[16,256]{1,0:T(8,128)S(1)}, u32[]{:S(2)}) copy-start(f32[16,256]{1,0:T(8,128)S(1)} %get-tuple-element.16) | copy-start | bytes 49156
  82.6 164.7 %copy-start.5 = (f32[256,16,20]{0,2,1:T(8,128)}, f32[256,16,20]{0,2,1:T(8,128)S(1)}, u32[]{:S(2)}) copy-start(f32[256,16,20]{0,2,1:T(8,128)S(1)} %reshape.113) | copy-start | bytes 983044
  248.7 2.9 collective-permute-start
  248.8 2.7 collective-permute-start.1
  251.5 5.7 %copy-start.20 = (f32[16]{0:T(128)}, f32[16]{0:T(128)S(1)}, u32[]{:S(2)}) copy-start(f32[16]{0:T(128)S(1)} %collective-permute-done.1) | copy-start | bytes 196
  254.6 31.3 %collective-permute-start.2 = (f32[16,128,128]{2,1,0:T(8,128)S(1)}, f32[16,128,128]{2,1,0:T(8,128)}, u32[]{:S(2)}, u32[]{:S(2)}) collective-permute-start(f32[16,128,128]{2,1,0:T(8,128)S(1)} %get-tuple-element.10), channel_id=1, source_target_pairs={{0,2},{2,0},{1,3},{3,1},{4,6},{6,4},{5,7},{7,5},{8,10},{10,8},{9,1... | collective-permute-start | bytes 3145736 | tf_op jit(solution)/shard_map/ppermute | solution.py:18
  256.7 23.8 %copy-start.24 = (f32[16]{0:T(128)}, f32[16]{0:T(128)S(1)}, u32[]{:S(2)}) copy-start(f32[16]{0:T(128)S(1)} %exponential_multiply_fusion) | copy-start | bytes 196
  256.7 23.2 %collective-permute-start.3 = (f32[16]{0:T(128)S(1)}, f32[16]{0:T(128)S(1)}, u32[]{:S(2)}, u32[]{:S(2)}) collective-permute-start(f32[16]{0:T(128)S(1)} %exponential_multiply_fusion), channel_id=1, source_target_pairs={{0,2},{2,0},{1,3},{3,1},{4,6},{6,4},{5,7},{7,5},{8,10},{10,8},{9,1... | collective-permute-start | bytes 200 | tf_op jit(solution)/shard_map/ppermute | solution.py:18
  258.0 25.3 %slice-start = ((f32[256,16,20]{0,2,1:T(8,128)}), f32[256,16,9]{0,2,1:T(8,128)S(1)}, s32[]{:S(2)}) async-start(f32[256,16,20]{0,2,1:T(8,128)} %copy-done.5), calls=%async_computation.4 | async-start | bytes 524288 | tf_op jit(solution)/shard_map/slice | solution.py:42
  285.9 5.4 %copy-start.3 = (f32[256,16,9]{2,1,0:T(8,128)S(1)}, f32[256,16,9]{2,1,0:T(8,128)}, u32[]{:S(2)}) copy-start(f32[256,16,9]{2,1,0:T(8,128)} %copy.51) | copy-start | bytes 442372
  285.9 5.4 %copy-start.9 = (f32[256,256]{1,0:T(8,128)S(1)}, f32[256,256]{1,0:T(8,128)}, u32[]{:S(2)}) copy-start(f32[256,256]{1,0:T(8,128)} %convolution_multiply_fusion) | copy-start | bytes 786436
  285.9 5.4 %copy-start.10 = (s32[256,256]{1,0:T(8,128)S(1)}, s32[256,256]{1,0:T(8,128)}, u32[]{:S(2)}) copy-start(s32[256,256]{1,0:T(8,128)} %convert_add_fusion) | copy-start | bytes 786436
  285.9 5.4 %copy-start.11 = (f32[16,256]{0,1:T(8,128)S(1)}, f32[16,256]{0,1:T(8,128)}, u32[]{:S(2)}) copy-start(f32[16,256]{0,1:T(8,128)} %copy.39) | copy-start | bytes 49156
  285.9 5.4 %copy-start.15 = (f32[16,256]{1,0:T(8,128)S(1)}, f32[16,256]{1,0:T(8,128)}, u32[]{:S(2)}) copy-start(f32[16,256]{1,0:T(8,128)} %copy-done.14) | copy-start | bytes 49156
  285.9 5.4 %copy-start.16 = (pred[256,256]{1,0:T(8,128)(4,1)S(1)}, pred[256,256]{1,0:T(8,128)(4,1)}, u32[]{:S(2)}) copy-start(pred[256,256]{1,0:T(8,128)(4,1)} %iota_compare_fusion.4) | copy-start | bytes 196612
  288.8 6.1 %copy-start.7 = (bf16[32,16,8,128]{3,2,1,0:T(8,128)(2,1)S(1)}, bf16[32,16,8,128]{3,2,1,0:T(8,128)(2,1)}, u32[]{:S(2)}) copy-start(bf16[32,16,8,128]{3,2,1,0:T(8,128)(2,1)} %copy-done.6) | copy-start | bytes 3145732
  288.8 48.7 %collective-permute-start.4 = (f32[16,128,128]{2,1,0:T(8,128)}, f32[16,128,128]{2,1,0:T(8,128)}, u32[]{:S(2)}, u32[]{:S(2)}) collective-permute-start(f32[16,128,128]{2,1,0:T(8,128)} %get-tuple-element.12), channel_id=1, source_target_pairs={{0,4},{4,0},{1,5},{5,1},{2,6},{6,2},{3,7},{7,3},{8,12},{12,8},{9,1... | collective-permute-start | bytes 3145736 | tf_op jit(solution)/shard_map/ppermute | solution.py:18
  297.2 3.8 %copy-start.2 = (bf16[16,128,128]{2,1,0:T(8,128)(2,1)S(1)}, bf16[16,128,128]{2,1,0:T(8,128)(2,1)}, u32[]{:S(2)}) copy-start(bf16[16,128,128]{2,1,0:T(8,128)(2,1)} %get-tuple-element.11) | copy-start | bytes 1572868
  301.0 36.5 %copy-start.19 = (f32[16]{0:T(128)S(1)}, f32[16]{0:T(128)}, u32[]{:S(2)}) copy-start(f32[16]{0:T(128)} %get-tuple-element.7) | copy-start | bytes 196
  (12 other events, 21.7 us)
Sparse Core Ops, SparseCore 0:
  9.2 29.2 all-gather.10
  40.3 39.4 all-gather.6
  81.7 157.2 all-gather.4
  248.9 26.6 all-gather.8
where the time goes:
time: 353 us; the launch traced here: 352 us
  waiting for transfers between devices  283 us (80%)
  matrix products  27.1 us (8%)
  other arithmetic  14.4 us (4%)
  between operations  13.5 us (4%)
  local copies, waits for them, and re-layouts  8.98 us (3%)
  starting transfers between devices  5.18 us (1%)
    all_gather x1, waiting for transfers between devices, per_device(): lax.all_gather(value_weight, 'dp', axis=0, tiled=True)  156 us
    ppermute x5, waiting for transfers between devices, from_partner(): return lax.ppermute(block, axis, route)  57.7 us
    all_gather x1, waiting for transfers between devices, per_device(): lax.all_gather(lambda_weight, 'dp', axis=0, tiled=True)  39.3 us
    all_gather x1, waiting for transfers between devices, per_device(): lax.all_gather(key_weight, 'dp', axis=0, tiled=True)  28.5 us
    dot_general x4, matrix products, accumulate(): jnp.dot(tokens, piece, preferred_element_type=jnp.float32)  14.8 us
    convert_element_type x3, other arithmetic, per_device(): carried = (carry_decay[:, None, None] * other_state).astype(jnp.bfloat16)  7.3 us
  transfers between devices with their start and end apart: 9, of which 6 were waited for; matrix products, arithmetic and copies ran while one was open for 8% of the time, Pallas kernels for 0%

commit v1 on v0

--- a/solution.py
+++ b/solution.py
@@ -1,11 +1,16 @@
+import functools
 import math
 
 import jax
 import jax.numpy as jnp
 from jax import lax
+from jax.experimental import pallas as pl
+from jax.experimental.pallas import tpu as pltpu
 from jax.sharding import PartitionSpec as P
 
 HIGHEST = lax.Precision.HIGHEST
+MESH = pl.DeviceIdType.MESH
+VMEM_LIMIT = 63 * 1024 * 1024
 
 
 def from_partner(block, axis, stride):
@@ -63,39 +68,220 @@
     )
 
 
-def make_fold(tokens):
-
-    def accumulate(totals, pieces, start):
-        return tuple(
-            (jnp.dot(tokens, piece, preferred_element_type=jnp.float32) for piece in pieces)
-        )
-
-    return accumulate
-
-
-def zeros_for(length, weights):
-    return tuple((jnp.zeros((length, weight.shape[1]), jnp.float32) for weight in weights))
+CHUNKS = 8
+SHARED = 2
+
+
+def gather_kernel(x_ref, a_ref, v_ref, qk_ref, lam_ref, val_ref, big_a, big_v, acc_a, acc_v,
+                  direct_sem, core_sem, send_sem, relay_sem, z_sem, fwd_sem):
+    depth = a_ref.shape[0]
+    rows = depth // CHUNKS
+    half = rows // 2
+    direct = CHUNKS - SHARED
+    dp = lax.axis_index("dp")
+    ctx = lax.axis_index("ctx")
+    x_at, y_at = dp % 2, dp // 2
+    core = ctx % 2
+    side = (ctx // 2) % 2
+    to_x = {"dp": y_at * 2 + (1 - x_at)}
+    to_y = {"dp": (1 - y_at) * 2 + x_at}
+    to_core = {"ctx": ctx + 1 - 2 * core}
+    to_z = {"ctx": ctx + 2 - 4 * side}
+    owners = (dp, y_at * 2 + (1 - x_at), (1 - y_at) * 2 + x_at, (1 - y_at) * 2 + (1 - x_at))
+
+    def place(i):
+        at = i + side * (CHUNKS - 1 - 2 * i)
+        return pl.ds(pl.multiple_of(at * rows + core * half, half), half)
+
+    pairs = ((a_ref, big_a), (v_ref, big_v))
+
+    def own_copy(way, i):
+        target = to_x if way == 0 else to_y
+        return [
+            pltpu.make_async_remote_copy(
+                src_ref=own.at[place(i)], dst_ref=big.at[way, place(i)],
+                send_sem=send_sem.at[way, i, k], recv_sem=direct_sem.at[way, i, k],
+                device_id=target, device_id_type=MESH)
+            for k, (own, big) in enumerate(pairs)]
+
+    def relay_copy(i):
+        way = 0 if i % 2 else 1
+        target = to_y if i % 2 else to_x
+        return [
+            pltpu.make_async_remote_copy(
+                src_ref=big.at[way, place(i)], dst_ref=big.at[2, place(i)],
+                send_sem=relay_sem.at[i, k], recv_sem=direct_sem.at[2, i, k],
+                device_id=target, device_id_type=MESH)
+            for k, (own, big) in enumerate(pairs)]
+
+    def z_copy(way, i):
+        return [
+            pltpu.make_async_remote_copy(
+                src_ref=big.at[way, place(i)], dst_ref=big.at[way, place(i)],
+                send_sem=z_sem.at[way, i, k], recv_sem=direct_sem.at[way, CHUNKS - 1 - i, k],
+                device_id=to_z, device_id_type=MESH)
+            for k, (own, big) in enumerate(pairs)]
+
+    def core_copy(way, i):
+        return [
+            pltpu.make_async_remote_copy(
+                src_ref=big.at[way, place(i)], dst_ref=big.at[way, place(i)],
+                send_sem=fwd_sem.at[way, i, k], recv_sem=core_sem.at[way, i, k],
+                device_id=to_core, device_id_type=MESH)
+            for k, (own, big) in enumerate(pairs)]
+
+    started = []
+
+    def start(copies):
+        for copy in copies:
+            copy.start()
+            started.append(copy)
+
+    def arrived(way, i):
+        for k, (own, big) in enumerate(pairs):
+            spot = big.at[way, place(i)]
+            pltpu.make_async_copy(spot, spot, direct_sem.at[way, i, k]).wait()
+
+    barrier = pltpu.get_barrier_semaphore()
+    for target in (to_x, to_y, to_core, to_z):
+        pl.semaphore_signal(barrier, inc=1, device_id=target, device_id_type=MESH)
+    pl.semaphore_wait(barrier, 4)
+
+    for i in range(2):
+        start(own_copy(0, i))
+        start(own_copy(1, i))
+
+    own_at = pl.ds(pl.multiple_of(owners[0] * depth, depth), depth)
+    tile = 512
+    wide = acc_v.shape[1]
+    acc_a[...] = jnp.dot(x_ref[:, own_at], a_ref[...], preferred_element_type=jnp.float32)
+
+    def first(n, carry):
+        cols = pl.ds(pl.multiple_of(n * tile, tile), tile)
+        acc_v[:, cols] = jnp.dot(
+            x_ref[:, own_at], v_ref[:, cols], preferred_element_type=jnp.float32)
+        return carry
+
+    lax.fori_loop(0, wide // tile, first, 0)
+
+    def multiply(way, pair):
+        span = 2 * rows
+        at = pair + side * (CHUNKS // 2 - 1 - 2 * pair)
+        low = pl.multiple_of(at * span, span)
+        for i in (2 * pair, 2 * pair + 1):
+            for k, (own, big) in enumerate(pairs):
+                at_i = i + side * (CHUNKS - 1 - 2 * i)
+                other = pl.ds(pl.multiple_of(at_i * rows + (1 - core) * half, half), half)
+                spot = big.at[way, other]
+                pltpu.make_async_copy(spot, spot, core_sem.at[way, i, k]).wait()
+        part = x_ref[:, pl.ds(pl.multiple_of(owners[way + 1] * depth + low, span), span)]
+        acc_a[...] += jnp.dot(
+            part, big_a[way, pl.ds(low, span)], preferred_element_type=jnp.float32)
+
+        def more(n, carry):
+            cols = pl.ds(pl.multiple_of(n * tile, tile), tile)
+            acc_v[:, cols] += jnp.dot(
+                part, big_v[way, pl.ds(low, span), cols], preferred_element_type=jnp.float32)
+            return carry
+
+        lax.fori_loop(0, wide // tile, more, 0)
+
+    ready = []
+
+    def take(way, i):
+        arrived(way, i)
+        if i < SHARED:
+            start(z_copy(way, i))
+        if way < 2 and i < direct and way == (0 if i % 2 else 1):
+            start(relay_copy(i))
+        start(core_copy(way, i))
+
+    seen = set()
+
+    def note(way, i):
+        take(way, i)
+        seen.add((way, i))
+        if (way, i ^ 1) in seen:
+            ready.append((way, i // 2))
+
+    lag = 2
+    for step in range(direct + lag):
+        if step < direct:
+            note(0, step)
+            note(1, step)
+            if step + 2 < direct:
+                start(own_copy(0, step + 2))
+                start(own_copy(1, step + 2))
+        if step >= lag:
+            back = step - lag
+            if back < SHARED:
+                note(0, CHUNKS - 1 - back)
+                note(1, CHUNKS - 1 - back)
+            note(2, back)
+        if step < direct and len(ready) > 1:
+            multiply(*ready.pop(0))
+    while len(ready) > 1:
+        multiply(*ready.pop(0))
+    for back in range(SHARED):
+        note(2, CHUNKS - 1 - back)
+    while ready:
+        multiply(*ready.pop(0))
+    for copy in started:
+        copy.wait_send()
+    narrow = qk_ref.shape[1]
+    qk_ref[...] = acc_a[:, :narrow].astype(jnp.bfloat16)
+    lam_ref[...] = jax.nn.softplus(acc_a[:, narrow:])
+    val_ref[...] = acc_v[...].astype(jnp.bfloat16)
+
+
+def project(tokens, query_weight, key_weight, value_weight, lambda_weight):
+    length = tokens.shape[0]
+    depth, wide = value_weight.shape
+    narrow = query_weight.shape[1] + key_weight.shape[1]
+    lams = lambda_weight.shape[1]
+    fill = -lams % 128
+    packed = jnp.concatenate(
+        (query_weight, key_weight, lambda_weight, jnp.zeros((depth, fill), jnp.bfloat16)), axis=1)
+    columns = packed.shape[1]
+    vmem = pl.BlockSpec(memory_space=pltpu.VMEM)
+    dma = pltpu.SemaphoreType.DMA
+    return pl.pallas_call(
+        gather_kernel,
+        out_shape=(
+            jax.ShapeDtypeStruct((length, narrow), jnp.bfloat16),
+            jax.ShapeDtypeStruct((length, lams + fill), jnp.float32),
+            jax.ShapeDtypeStruct((length, wide), jnp.bfloat16),
+        ),
+        in_specs=[vmem] * 3,
+        out_specs=(vmem,) * 3,
+        scratch_shapes=[
+            pltpu.VMEM((3, depth, columns), jnp.bfloat16),
+            pltpu.VMEM((3, depth, wide), jnp.bfloat16),
+            pltpu.VMEM((length, columns), jnp.float32),
+            pltpu.VMEM((length, wide), jnp.float32),
+            dma((3, CHUNKS, 2)),
+            dma((3, CHUNKS, 2)),
+            dma((2, CHUNKS, 2)),
+            dma((CHUNKS, 2)),
+            dma((3, SHARED, 2)),
+            dma((3, CHUNKS, 2)),
+        ],
+        compiler_params=pltpu.CompilerParams(
+            collective_id=0, has_side_effects=True, vmem_limit_bytes=VMEM_LIMIT),
+        name="gather_project",
+    )(tokens, packed, value_weight)
 
 
 def per_device(inputs, query_weight, key_weight, value_weight, lambda_weight, log_decay, norm_gain):
     tokens = inputs[0]
     decays = log_decay[0]
     length = tokens.shape[0]
-    accumulate = make_fold(tokens)
-    query_sum, key_sum, value_sum, lambda_sum = accumulate(
-        zeros_for(length, (query_weight, key_weight, value_weight, lambda_weight)),
-        (
-            lax.all_gather(query_weight, "dp", axis=0, tiled=True),
-            lax.all_gather(key_weight, "dp", axis=0, tiled=True),
-            lax.all_gather(value_weight, "dp", axis=0, tiled=True),
-            lax.all_gather(lambda_weight, "dp", axis=0, tiled=True),
-        ),
-        jnp.int32(0),
-    )
-    query_rows = query_sum.astype(jnp.bfloat16)
-    key_rows = key_sum.astype(jnp.bfloat16)
-    value_rows = value_sum.astype(jnp.bfloat16)
-    lambdas = jax.nn.softplus(lambda_sum)
+    qk, lambdas, value_rows = project(
+        tokens, query_weight, key_weight, value_weight, lambda_weight)
+    state_dim = query_weight.shape[1]
+    query_rows = qk[:, :state_dim]
+    key_rows = qk[:, state_dim:]
+    lambdas = lambdas[:, :lambda_weight.shape[1]]
     masks = level_masks(length)
     inner = masks.shape[0]
     scale = 1.0 / math.sqrt(query_rows.shape[1])
@@ -110,7 +296,9 @@
     growth = jnp.exp(cumulative)
     mixed = near
     for level_bit in range(bits):
-        other_state, other_total = from_partner((block_state, block_total), "ctx", level_bit)
+        other_state, other_total = from_partner(
+            (block_state.astype(jnp.bfloat16), block_total), "ctx", level_bit)
+        other_state = other_state.astype(jnp.float32)
         upper = (index >> level_bit & 1).astype(jnp.float32)
         carried = (carry_decay[:, None, None] * other_state).astype(jnp.bfloat16)
         reach = jnp.einsum("ts,hsd->thd", query_rows, carried, preferred_element_type=jnp.float32)

time: 353 us -> 165 us (0.47)
  waiting for transfers between devices: 283 us -> 28.7 us
  Pallas kernels: 0 us -> 89.9 us
  between operations: 13.5 us -> 0.25 us
  matrix products: 27.1 us -> 14.5 us
    all_gather x4 -> x0, waiting for transfers between devices: 224 us -> none  [the longest x1 156 us: per_device(): lax.all_gather(value_weight, 'dp', axis=0, tiled=True)]
    pallas_call x0 -> x1, Pallas kernels: none -> 89.9 us  [project(): pl.pallas_call(gather_kernel, out_shape=(jax.ShapeDtypeStruct((length, na...]
    ppermute x5, waiting for transfers between devices: 57.7 us -> 28.7 us  [from_partner(): return lax.ppermute(block, axis, route)]
    dot_general x4 -> x0, matrix products: 14.8 us -> none  [accumulate(): jnp.dot(tokens, piece, preferred_element_type=jnp.float32)]
    convert_element_type x3 -> x2, other arithmetic: 7.3 us -> 2.37 us  [per_device(): carried = (carry_decay[:, None, None] * other_state).astype(jnp.bfloat16)]
  transfers between devices with their start and end apart: 9 -> 5, of which waited for: 6 -> 2; matrix products, arithmetic and copies ran while one was open for 8% -> 16% of each run, Pallas kernels for 0% -> 55%
where the time goes in v1:
time: 165 us; the launch traced here: 164 us
  Pallas kernels  89.9 us (54%)
  waiting for transfers between devices  28.7 us (17%)
  other arithmetic  14.6 us (9%)
  matrix products  14.5 us (9%)
  local copies, waits for them, and re-layouts  10.3 us (6%)
  starting transfers between devices  6.05 us (4%)
    pallas_call x1, Pallas kernels, project(): pl.pallas_call(gather_kernel, out_shape=(jax.ShapeDtypeStruct((length, na...  89.9 us
    ppermute x5, waiting for transfers between devices, from_partner(): return lax.ppermute(block, axis, route)  28.7 us
    dot_general x1, matrix products, block_terms(): jnp.einsum('lts,thl->hts', masks, weights_all[:, :, :inner], precision=HI...  6.24 us
    ppermute x5, starting transfers between devices, from_partner(): return lax.ppermute(block, axis, route)  6.05 us
    unnamed x28, local copies, waits for them, and re-layouts  5.51 us
    unnamed x3, matrix products  3.94 us
    reduce_sum x1, other arithmetic, finish(): mean_square = jnp.mean(mixed * mixed, axis=-1, keepdims=True)  3.31 us
  transfers between devices with their start and end apart: 5, of which 2 were waited for; matrix products, arithmetic and copies ran while one was open for 16% of the time, Pallas kernels for 55%

profile of v1, /device:TPU:0, one launch (start us, length us, event | category | flops | bytes accessed | tf_op | source)
XLA Modules:
  0.0 164.4 jit_solution(6105806687751945393)
XLA Ops:
  0.0 0.7 copy-done
  3.5 1.4 copy.39
  5.0 2.4 %maximum_maximum_fusion.a_ref = bf16[1024,640]{1,0:T(8,128)(2,1)} fusion(bf16[1024,320]{1,0:T(8,128)(2,1)S(1)} %copy.39, bf16[1024,128]{1,0:T(8,128)(2,1)} %param.9, bf16[1024,128]{1,0:T(8,128)(2,1)} %param.8, bf16[640]{0:T(1024)(128)(2,1)S(1)} %pad.3.clone), kind=kLoop, calls=%fused_computation.19 | loop fusion | flops 5242880 | bytes 2491648 | tf_op jit(solution)/shard_map/concatenate | solution.py:243
  7.4 89.9 %gather_project.1 = (bf16[256,256]{1,0:T(8,128)(2,1)}, f32[256,384]{1,0:T(8,128)}, bf16[256,2048]{1,0:T(8,128)(2,1)}) custom-call(bf16[256,4096]{1,0:T(8,128)(2,1)} %bitcast.102, bf16[1024,640]{1,0:T(8,128)(2,1)} %maximum_maximum_fusion.a_ref, bf16[1024,2048]{1,0:T(8,128)(2,1)} %v_ref.1), custom_call_target="tpu_custom_call" | custom-call | tf_op jit(solution)/shard_map/gather_project/pallas_call | solution.py:248
  97.3 1.2 copy.40
  98.6 0.9 slice_convert_fusion
  99.6 0.7 fusion.40
  100.3 1.2 fusion.46
  101.5 0.9 collective-permute-start
  102.5 0.9 convolution_multiply_fusion
  104.0 2.5 %copy.56 = f32[256,16,9]{2,1,0:T(8,128)} copy(f32[256,16,9]{0,2,1:T(8,128)S(1)} %slice.41) | data formatting | bytes 294912
  106.7 6.2 %fusion.1 = bf16[16,256,256]{2,0,1:T(8,128)(2,1)} fusion(f32[256,16,9]{2,1,0:T(8,128)} %copy.56, f32[256,256]{1,0:T(8,128)S(1)} %copy-done.5, f32[16,256]{1,0:T(8,128)} %get-tuple-element.20, f32[16,256]{0,1:T(8,128)S(1)} %copy.44, s32[256,256]{1,0:T(8,128)S(1)} %convert_add_fusion.2, pred[256,256]{1,0:T(8,128)(4,1)} %iota_compare_fusion.4), kind=kOutput, calls=%fused_computation.2 | convolution fusion | flops 119078912 | bytes 2867200 | tf_op jit(solution)/shard_map/lts,thl->hts/dot_general | solution.py:47
  113.0 2.0 %fusion.43 = bf16[16,128,128]{2,1,0:T(8,128)(2,1)} fusion(f32[16,128,128]{2,1,0:T(8,128)S(1)} %get-tuple-element.27, f32[16]{0:T(128)} %collective-permute-done.1, bf16[16,128,128]{2,1,0:T(8,128)(2,1)S(1)} %collective-permute-done, f32[16]{0:T(128)} %exp.19, pred[]{:T(512)S(6)} %gt.8), kind=kLoop, calls=%fused_computation.74 | loop fusion | flops 1835008 | bytes 2097281 | tf_op jit(solution)/shard_map/convert_element_type | solution.py:300
  115.5 2.3 %fusion.5 = f32[16,128,256]{2,1,0:T(8,128)} fusion(bf16[16,256,256]{2,0,1:T(8,128)(2,1)S(1)} %copy-done.3, bf16[256,2048]{1,0:T(8,128)(2,1)S(1)} %copy-done.2), kind=kOutput, calls=%fused_computation.8 | convolution fusion | flops 268435456 | bytes 5242880 | tf_op jit(solution)/shard_map/hts,shd->thd/dot_general | solution.py:55
  118.4 1.4 collective-permute-start.3
  119.9 9.2 %collective-permute-done.3 = f32[16]{0:T(128)S(1)} collective-permute-done((f32[16]{0:T(128)S(1)}, f32[16]{0:T(128)S(1)}, u32[]{:S(2)}, u32[]{:S(2)}) %collective-permute-start.3) | collective-permute-done | bytes 96 | tf_op jit(solution)/shard_map/ppermute | solution.py:23
  129.4 2.2 %fusion.10 = (bf16[16,128,128]{2,1,0:T(8,128)(2,1)S(1)}, bf16[16,128,128]{2,1,0:T(8,128)(2,1)}) fusion(bf16[16,128,128]{2,1,0:T(8,128)(2,1)S(1)} %collective-permute-done.2, f32[16]{0:T(128)S(1)} %get-tuple-element.14, f32[16]{0:T(128)S(1)} %collective-permute-done.3, f32[16,128,128]{2,1,0:T(8,128)S(1)} %get-tuple-element.27, f32[16]{0:T(128)} %collective-permute-done.1, ...), kind=kLoop, calls=%fused_computation.23 | loop fusion | flops 3932160 | bytes 3146050 | tf_op jit(solution)/shard_map/convert_element_type | solution.py:303
  131.6 2.6 %collective-permute-start.4 = (bf16[16,128,128]{2,1,0:T(8,128)(2,1)}, bf16[16,128,128]{2,1,0:T(8,128)(2,1)S(1)}, u32[]{:S(2)}, u32[]{:S(2)}) collective-permute-start(bf16[16,128,128]{2,1,0:T(8,128)(2,1)} %get-tuple-element.16), channel_id=1, source_target_pairs={{0,4},{4,0},{1,5},{5,1},{2,6},{6,2},{3,7},{7,3},{8,12},{12,8},{9,1... | collective-permute-start | bytes 1572872 | tf_op jit(solution)/shard_map/ppermute | solution.py:23
  134.2 1.8 %fusion.34 = f32[256,2048]{0,1} fusion(bf16[128,2048]{0,1:T(8,128)(2,1)S(1)} %bitcast.99, bf16[256,256]{1,0:T(8,128)(2,1)S(1)} %copy-done.4), kind=kOutput, calls=%fused_computation.52 | convolution fusion | flops 134217728 | bytes 2686976
  136.2 1.8 %fusion.32 = f32[256,2048]{0,1} fusion(bf16[128,2048]{0,1:T(8,128)(2,1)S(1)} %bitcast.101, bf16[256,256]{1,0:T(8,128)(2,1)S(1)} %copy-done.4), kind=kOutput, calls=%fused_computation.50 | convolution fusion | flops 134217728 | bytes 2686976
  138.0 19.5 %collective-permute-done.4 = bf16[16,128,128]{2,1,0:T(8,128)(2,1)S(1)} collective-permute-done((bf16[16,128,128]{2,1,0:T(8,128)(2,1)}, bf16[16,128,128]{2,1,0:T(8,128)(2,1)S(1)}, u32[]{:S(2)}, u32[]{:S(2)}) %collective-permute-start.4) | collective-permute-done | bytes 524320 | tf_op jit(solution)/shard_map/ppermute | solution.py:23
  158.4 0.8 copy-done.1
  159.2 3.3 %multiply_reduce_fusion = (f32[256,16]{0,1:T(8,128)S(1)}, f32[256,16,128]{0,2,1:T(8,128)S(1)}) fusion(f32[256,16]{0,1:T(8,128)S(1)} %copy-done.8, f32[256,16]{0,1:T(8,128)S(1)} %copy-done.7, f32[256,16]{0,1:T(8,128)S(1)} %copy-done.6, f32[16,128,256]{2,1,0:T(8,128)S(1)} %copy-done.1, f32[256,2048]{0,1:S(1)} %fusion.30, f32[256,2048]{0,1} %fusion.32, ...), kind=kLoop, calls=%fused_computation.11 | loop fusion | flops 4190208 | bytes 10551296 | tf_op jit(solution)/shard_map/reduce_sum | solution.py:65
  162.9 1.4 copy.54
  (55 shorter events, 6.9 us)
Async XLA Ops:
  0.0 0.7 copy-start
  2.4 97.2 %copy-start.11 = (f32[16]{0:T(128)}, f32[16]{0:T(128)S(1)}, u32[]{:S(2)}) copy-start(f32[16]{0:T(128)S(1)} %slice_reduce_fusion.1) | copy-start | bytes 196
  3.0 110.0 %collective-permute-start.1 = (f32[16]{0:T(128)}, f32[16]{0:T(128)}, u32[]{:S(2)}, u32[]{:S(2)}) collective-permute-start(f32[16]{0:T(128)} %exp.19), channel_id=1, source_target_pairs={{0,1},{1,0},{2,3},{3,2},{4,5},{5,4},{6,7},{7,6},{8,9},{9,8},{10,11... | collective-permute-start | bytes 200 | tf_op jit(solution)/shard_map/ppermute | solution.py:23
  97.3 3.0 %copy-start.2 = (bf16[256,2048]{1,0:T(8,128)(2,1)S(1)}, bf16[256,2048]{1,0:T(8,128)(2,1)}, u32[]{:S(2)}) copy-start(bf16[256,2048]{1,0:T(8,128)(2,1)} %get-tuple-element.8) | copy-start | bytes 3145732
  98.5 3.9 %copy-start.4 = (bf16[256,256]{1,0:T(8,128)(2,1)S(1)}, bf16[256,256]{1,0:T(8,128)(2,1)}, u32[]{:S(2)}) copy-start(bf16[256,256]{1,0:T(8,128)(2,1)} %get-tuple-element.10) | copy-start | bytes 393220
  101.5 5.0 %copy-start.9 = (f32[16,256]{1,0:T(8,128)S(1)}, f32[16,256]{1,0:T(8,128)}, u32[]{:S(2)}) copy-start(f32[16,256]{1,0:T(8,128)} %get-tuple-element.20) | copy-start | bytes 49156
  101.5 11.4 %collective-permute-start = (bf16[16,128,128]{2,1,0:T(8,128)(2,1)}, bf16[16,128,128]{2,1,0:T(8,128)(2,1)S(1)}, u32[]{:S(2)}, u32[]{:S(2)}) collective-permute-start(bf16[16,128,128]{2,1,0:T(8,128)(2,1)} %get-tuple-element.26), channel_id=1, source_target_pairs={{0,1},{1,0},{2,3},{3,2},{4,5},{5,4},{6,7},{7,6},{8,9},{9,8},{10,11... | collective-permute-start | bytes 1572872 | tf_op jit(solution)/shard_map/ppermute | solution.py:23
  104.0 2.7 %copy-start.5 = (f32[256,256]{1,0:T(8,128)S(1)}, f32[256,256]{1,0:T(8,128)}, u32[]{:S(2)}) copy-start(f32[256,256]{1,0:T(8,128)} %convolution_multiply_fusion) | copy-start | bytes 786436
  113.0 2.6 %copy-start.3 = (bf16[16,256,256]{2,0,1:T(8,128)(2,1)S(1)}, bf16[16,256,256]{2,0,1:T(8,128)(2,1)}, u32[]{:S(2)}) copy-start(bf16[16,256,256]{2,0,1:T(8,128)(2,1)} %fusion.1) | copy-start | bytes 6291460
  114.9 2.8 %copy-start.12 = (f32[16]{0:T(128)S(1)}, f32[16]{0:T(128)}, u32[]{:S(2)}) copy-start(f32[16]{0:T(128)} %copy-done.11) | copy-start | bytes 196
  114.9 14.4 %collective-permute-start.2 = (bf16[16,128,128]{2,1,0:T(8,128)(2,1)}, bf16[16,128,128]{2,1,0:T(8,128)(2,1)S(1)}, u32[]{:S(2)}, u32[]{:S(2)}) collective-permute-start(bf16[16,128,128]{2,1,0:T(8,128)(2,1)} %fusion.43), channel_id=1, source_target_pairs={{0,2},{2,0},{1,3},{3,1},{4,6},{6,4},{5,7},{7,5},{8,10},{10,8},{9,1... | collective-permute-start | bytes 1572872 | tf_op jit(solution)/shard_map/ppermute | solution.py:23
  118.4 10.7 %collective-permute-start.3 = (f32[16]{0:T(128)S(1)}, f32[16]{0:T(128)S(1)}, u32[]{:S(2)}, u32[]{:S(2)}) collective-permute-start(f32[16]{0:T(128)S(1)} %exponential_multiply_fusion), channel_id=1, source_target_pairs={{0,2},{2,0},{1,3},{3,1},{4,6},{6,4},{5,7},{7,5},{8,10},{10,8},{9,1... | collective-permute-start | bytes 200 | tf_op jit(solution)/shard_map/ppermute | solution.py:23
  131.6 25.9 %collective-permute-start.4 = (bf16[16,128,128]{2,1,0:T(8,128)(2,1)}, bf16[16,128,128]{2,1,0:T(8,128)(2,1)S(1)}, u32[]{:S(2)}, u32[]{:S(2)}) collective-permute-start(bf16[16,128,128]{2,1,0:T(8,128)(2,1)} %get-tuple-element.16), channel_id=1, source_target_pairs={{0,4},{4,0},{1,5},{5,1},{2,6},{6,2},{3,7},{7,3},{8,12},{12,8},{9,1... | collective-permute-start | bytes 1572872 | tf_op jit(solution)/shard_map/ppermute | solution.py:23
  157.6 1.6 copy-start.1
  157.6 1.6 copy-start.6
  157.6 1.6 copy-start.7
  157.7 1.6 copy-start.8
  159.2 3.3 %copy-start.10 = (f32[2048]{0:T(1024)S(1)}, f32[2048]{0:T(1024)}, u32[]{:S(2)}) copy-start(f32[2048]{0:T(1024)} %param.13) | copy-start | bytes 24580

commit v2 on v1

--- a/solution.py
+++ b/solution.py
@@ -11,61 +11,6 @@
 HIGHEST = lax.Precision.HIGHEST
 MESH = pl.DeviceIdType.MESH
 VMEM_LIMIT = 63 * 1024 * 1024
-
-
-def from_partner(block, axis, stride):
-    count = lax.axis_size(axis)
-    route = []
-    for low in range(count):
-        high = low | 1 << stride
-        if high != low and high < count:
-            route += [(low, high), (high, low)]
-    return lax.ppermute(block, axis, route)
-
-
-def level_masks(length):
-    depth = length.bit_length() - 1
-    token_place = jnp.arange(length, dtype=jnp.int32)
-    differ = jnp.bitwise_xor(token_place[:, None], token_place[None, :])
-    level = jnp.zeros((length, length), jnp.int32)
-    for power in range(depth):
-        level = level + (differ >= 1 << power).astype(jnp.int32)
-    levels = jnp.arange(depth + 1, dtype=jnp.int32)
-    return (level[None, :, :] == levels[:, None, None]).astype(jnp.float32)
-
-
-def block_terms(query_rows, key_rows, value_rows, lambdas, log_decay, masks):
-    length, heads = log_decay.shape
-    state_dim = query_rows.shape[1]
-    head_dim = value_rows.shape[1] // heads
-    inner = masks.shape[0]
-    weights_all = lambdas.reshape(length, heads, -1)
-    cumulative = jnp.cumsum(log_decay, axis=0)
-    scores = lax.dot_general(
-        query_rows, key_rows, (((1,), (1,)), ((), ())), preferred_element_type=jnp.float32
-    ) / math.sqrt(state_dim)
-    level_weight = jnp.einsum("lts,thl->hts", masks, weights_all[:, :, :inner], precision=HIGHEST)
-    token_place = jnp.arange(length, dtype=jnp.int32)
-    causal = token_place[:, None] >= token_place[None, :]
-    spread = jnp.transpose(cumulative)
-    distance = spread[:, :, None] - spread[:, None, :]
-    decay = jnp.exp(jnp.where(causal[None], distance, -jnp.inf))
-    mix = (level_weight * decay * scores[None]).astype(jnp.bfloat16)
-    values = value_rows.reshape(length, heads, head_dim)
-    near = jnp.einsum("hts,shd->thd", mix, values, preferred_element_type=jnp.float32)
-    remain = jnp.exp(cumulative[-1][None, :] - cumulative)
-    keyed = (key_rows.astype(jnp.float32)[:, None, :] * remain[:, :, None]).astype(jnp.bfloat16)
-    state = jnp.einsum("chs,chd->hsd", keyed, values, preferred_element_type=jnp.float32)
-    total = jnp.exp(cumulative[-1])
-    return (near, state, total, cumulative, weights_all)
-
-
-def finish(mixed, norm_gain):
-    heads = mixed.shape[-2]
-    mean_square = jnp.mean(mixed * mixed, axis=-1, keepdims=True)
-    return (mixed * lax.rsqrt(mean_square + 1e-05) * norm_gain.reshape(heads, -1)).astype(
-        jnp.bfloat16
-    )
 
 
 CHUNKS = 8
@@ -272,47 +217,236 @@
     )(tokens, packed, value_weight)
 
 
+def flipped(index, mask):
+    out = index
+    for power in range(mask.bit_length()):
+        if mask >> power & 1:
+            step = 1 << power
+            out = out + step - 2 * step * ((index // step) % 2)
+    return out
+
+
+def mixer_kernel(levels, qk_ref, lam_ref, val_ref, decay_ref, gain_ref, out_ref, logs, state,
+                 sent, got, mixed, score, cum, grow, log_send, log_recv, first_send, first_recv,
+                 part_send, part_recv, share_send, share_recv):
+    count = lax.axis_size("ctx")
+    bits = count.bit_length() - 1
+    ctx = lax.axis_index("ctx")
+    length, heads = decay_ref.shape
+    head_dim = val_ref.shape[1] // heads
+    state_dim = qk_ref.shape[1] // 2
+    inner = length.bit_length()
+    scale = 1.0 / math.sqrt(state_dim)
+    tile = 128
+    tiles = length // tile
+    peers = [None] + [{"ctx": flipped(ctx, r)} for r in range(1, count)]
+    started = []
+
+    def send(src, dst, out_sem, in_sem, peer):
+        copy = pltpu.make_async_remote_copy(
+            src_ref=src, dst_ref=dst, send_sem=out_sem, recv_sem=in_sem,
+            device_id=peers[peer], device_id_type=MESH)
+        copy.start()
+        started.append(copy)
+
+    def await_at(spot, sem):
+        pltpu.make_async_copy(spot, spot, sem).wait()
+
+    barrier = pltpu.get_barrier_semaphore()
+    for r in range(1, count):
+        pl.semaphore_signal(barrier, inc=1, device_id=peers[r], device_id_type=MESH)
+
+    row = lax.broadcasted_iota(jnp.int32, (length, length), 0)
+    col = lax.broadcasted_iota(jnp.int32, (length, length), 1)
+    below = (row >= col).astype(jnp.float32)
+    decays = decay_ref[...]
+    ones = jnp.ones((length, tile), jnp.float32)
+    logs[0] = lax.dot_general(
+        decays, ones, (((0,), (0,)), ((), ())), precision=HIGHEST,
+        preferred_element_type=jnp.float32)
+    cum_col = jnp.dot(below, decays, precision=HIGHEST, preferred_element_type=jnp.float32)
+    cum_row = lax.dot_general(
+        decays, below, (((0,), (1,)), ((), ())), precision=HIGHEST,
+        preferred_element_type=jnp.float32)
+    cum[...] = cum_row
+    grow[...] = jnp.exp(cum_col) * scale
+    remain = jnp.exp(cum_col[length - 1:length] - cum_col)
+    pl.semaphore_wait(barrier, count - 1)
+    for r in range(1, count):
+        send(logs.at[0], logs.at[r], log_send.at[r], log_recv.at[r], r)
+
+    def values_of(h):
+        return val_ref[:, h * head_dim:(h + 1) * head_dim]
+
+    keys = qk_ref[:, state_dim:].astype(jnp.float32)
+    halves = 2
+    for part in range(halves):
+        span = heads // halves
+        for h in range(part * span, (part + 1) * span):
+            keyed = (keys * remain[:, h:h + 1]).astype(jnp.bfloat16)
+            block = lax.dot_general(
+                keyed, values_of(h), (((0,), (0,)), ((), ())),
+                preferred_element_type=jnp.float32)
+            state[h] = block
+            sent[0, h] = block.astype(jnp.bfloat16)
+        if bits > 0:
+            at = pl.ds(part * span, span)
+            send(sent.at[0, at], got.at[0, at], first_send.at[part], first_recv.at[part], 1)
+
+    trow = lax.broadcasted_iota(jnp.int32, (tile, tile), 0)
+    tcol = lax.broadcasted_iota(jnp.int32, (tile, tile), 1)
+    differ = jnp.bitwise_xor(trow, tcol)
+    depth = tile.bit_length() - 1
+    full = lax.dot_general(
+        qk_ref[:, :state_dim], qk_ref[:, state_dim:], (((1,), (1,)), ((), ())),
+        preferred_element_type=jnp.float32)
+    score[...] = jnp.where(row >= col, full * scale, 0.0)
+
+    def near(h):
+        base = h * levels
+        for ti in range(tiles):
+            rows = slice(ti * tile, (ti + 1) * tile)
+            total = None
+            for tj in range(ti + 1):
+                cols = slice(tj * tile, (tj + 1) * tile)
+                if ti == tj:
+                    weight = jnp.broadcast_to(lam_ref[rows, base:base + 1], (tile, tile))
+                    for level in range(1, depth + 1):
+                        at = base + level
+                        weight = jnp.where(
+                            differ >= 1 << (level - 1), lam_ref[rows, at:at + 1], weight)
+                else:
+                    at = base + depth + (ti ^ tj).bit_length()
+                    weight = lam_ref[rows, at:at + 1]
+                distance = cum_col[rows, h:h + 1] - cum[h:h + 1, cols]
+                decay = jnp.exp(jnp.minimum(distance, 0.0))
+                mix = (weight * (decay * score[rows, cols])).astype(jnp.bfloat16)
+                term = jnp.dot(
+                    mix, val_ref[cols, h * head_dim:(h + 1) * head_dim],
+                    preferred_element_type=jnp.float32)
+                total = term if total is None else total + term
+            mixed[rows, h * head_dim:(h + 1) * head_dim] = total
+
+    left = list(range(heads))
+
+    def near_some(most):
+        for _ in range(min(most, len(left))):
+            near(left.pop(0))
+
+    def far(b, h, carry, upper):
+        carried = (carry[h:h + 1] * got[b, h].astype(jnp.float32)).astype(jnp.bfloat16)
+        reach = jnp.dot(qk_ref[:, :state_dim], carried, preferred_element_type=jnp.float32)
+        at = h * levels + inner + b
+        factor = lam_ref[:, at:at + 1] * grow[:, h:h + 1] * upper
+        return factor * reach
+
+    near_some(3)
+    for r in range(1, count):
+        await_at(logs.at[r], log_recv.at[r])
+    own_log = logs[0]
+    carry_log = jnp.zeros_like(own_log)
+    pending = []
+    for b in range(bits):
+        upper = ((ctx // (1 << b)) % 2).astype(jnp.float32)
+        other_log = logs[1 << b]
+        for r in range((1 << b) + 1, 2 << b):
+            other_log = other_log + logs[r]
+        group = min(1 << b, 4)
+        if b == 0:
+            for part in range(halves):
+                at = pl.ds(part * (heads // halves), heads // halves)
+                await_at(got.at[0, at], first_recv.at[part])
+        else:
+            span = heads // group
+
+            def slot(ref, r):
+                return ref.at[b, pl.ds(flipped(ctx % group, r) * span, span)]
+
+            await_at(slot(got, 0), part_recv.at[b])
+            for r in range(1, group):
+                send(slot(got, 0), slot(got, 0), share_send.at[b, r], share_recv.at[b, r], r)
+            near_some(2)
+            if b + 1 == bits:
+                near_some(heads)
+                for p in pending:
+                    for h in range(heads):
+                        cols = slice(h * head_dim, (h + 1) * head_dim)
+                        mixed[:, cols] += far(p[0], h, p[1], p[2])
+            for r in range(1, group):
+                await_at(slot(got, r), share_recv.at[b, r])
+        pending.append((b, jnp.exp(carry_log), upper))
+        if b + 1 < bits:
+            keep = jnp.where(upper > 0, 1.0, jnp.exp(other_log))
+            take = jnp.where(upper > 0, jnp.exp(own_log), 1.0)
+            for h in range(heads):
+                block = keep[h:h + 1] * state[h] + take[h:h + 1] * got[b, h].astype(jnp.float32)
+                state[h] = block
+                sent[b + 1, h] = block.astype(jnp.bfloat16)
+            ahead = min(2 << b, 4)
+            wide = heads // ahead
+            at = pl.ds((ctx % ahead) * wide, wide)
+            send(sent.at[b + 1, at], got.at[b + 1, at], part_send.at[b + 1],
+                 part_recv.at[b + 1], 2 << b)
+            carry_log = carry_log + upper * other_log
+            own_log = own_log + other_log
+            near_some(5)
+    near_some(heads)
+    rest = pending[-1:] if bits > 1 else pending
+    for h in range(heads):
+        cols = slice(h * head_dim, (h + 1) * head_dim)
+        whole = mixed[:, cols]
+        for p in rest:
+            whole = whole + far(p[0], h, p[1], p[2])
+        mean_square = jnp.mean(whole * whole, axis=-1, keepdims=True)
+        out_ref[:, cols] = (whole * lax.rsqrt(mean_square + 1e-05) * gain_ref[:, cols]).astype(
+            jnp.bfloat16)
+    for copy in started:
+        copy.wait_send()
+
+
+def mix_all(qk, lambdas, value_rows, decays, norm_gain, levels):
+    length, heads = decays.shape
+    wide = value_rows.shape[1]
+    state_dim = qk.shape[1] // 2
+    head_dim = wide // heads
+    count = lax.axis_size("ctx")
+    bits = count.bit_length() - 1
+    vmem = pl.BlockSpec(memory_space=pltpu.VMEM)
+    dma = pltpu.SemaphoreType.DMA
+    return pl.pallas_call(
+        functools.partial(mixer_kernel, levels),
+        out_shape=jax.ShapeDtypeStruct((length, wide), jnp.bfloat16),
+        in_specs=[vmem] * 5,
+        out_specs=vmem,
+        scratch_shapes=[
+            pltpu.VMEM((count, heads, 128), jnp.float32),
+            pltpu.VMEM((heads, state_dim, head_dim), jnp.float32),
+            pltpu.VMEM((bits, heads, state_dim, head_dim), jnp.bfloat16),
+            pltpu.VMEM((bits, heads, state_dim, head_dim), jnp.bfloat16),
+            pltpu.VMEM((length, wide), jnp.float32),
+            pltpu.VMEM((length, length), jnp.float32),
+            pltpu.VMEM((heads, length), jnp.float32),
+            pltpu.VMEM((length, heads), jnp.float32),
+            dma((count,)),
+            dma((count,)),
+            dma((2,)),
+            dma((2,)),
+            dma((bits,)),
+            dma((bits,)),
+            dma((bits, 4)),
+            dma((bits, 4)),
+        ],
+        compiler_params=pltpu.CompilerParams(
+            collective_id=1, has_side_effects=True, vmem_limit_bytes=VMEM_LIMIT),
+        name="mixer",
+    )(qk, lambdas, value_rows, decays, norm_gain[None])
+
+
 def per_device(inputs, query_weight, key_weight, value_weight, lambda_weight, log_decay, norm_gain):
-    tokens = inputs[0]
-    decays = log_decay[0]
-    length = tokens.shape[0]
     qk, lambdas, value_rows = project(
-        tokens, query_weight, key_weight, value_weight, lambda_weight)
-    state_dim = query_weight.shape[1]
-    query_rows = qk[:, :state_dim]
-    key_rows = qk[:, state_dim:]
-    lambdas = lambdas[:, :lambda_weight.shape[1]]
-    masks = level_masks(length)
-    inner = masks.shape[0]
-    scale = 1.0 / math.sqrt(query_rows.shape[1])
-    near, state, total, cumulative, weights_all = block_terms(
-        query_rows, key_rows, value_rows, lambdas, decays, masks
-    )
-    index = lax.axis_index("ctx")
-    bits = lax.axis_size("ctx").bit_length() - 1
-    block_state = state
-    block_total = total
-    carry_decay = jnp.ones_like(total)
-    growth = jnp.exp(cumulative)
-    mixed = near
-    for level_bit in range(bits):
-        other_state, other_total = from_partner(
-            (block_state.astype(jnp.bfloat16), block_total), "ctx", level_bit)
-        other_state = other_state.astype(jnp.float32)
-        upper = (index >> level_bit & 1).astype(jnp.float32)
-        carried = (carry_decay[:, None, None] * other_state).astype(jnp.bfloat16)
-        reach = jnp.einsum("ts,hsd->thd", query_rows, carried, preferred_element_type=jnp.float32)
-        factor = weights_all[:, :, inner + level_bit] * growth * (scale * upper)
-        mixed = mixed + factor[..., None] * reach
-        if level_bit + 1 < bits:
-            block_state = jnp.where(
-                upper > 0,
-                block_total[:, None, None] * other_state + block_state,
-                other_total[:, None, None] * block_state + other_state,
-            )
-            carry_decay = jnp.where(upper > 0, other_total * carry_decay, carry_decay)
-            block_total = block_total * other_total
-    return finish(mixed, norm_gain).reshape(1, length, -1)
+        inputs[0], query_weight, key_weight, value_weight, lambda_weight)
+    levels = lambda_weight.shape[1] // log_decay.shape[2]
+    return mix_all(qk, lambdas, value_rows, log_decay[0], norm_gain, levels)[None]
 
 
 def solution(mesh):

time: 165 us -> 133 us (0.81)
  Pallas kernels: 89.9 us -> 126 us
  waiting for transfers between devices: 28.7 us -> 0 us
  matrix products: 14.5 us -> 0 us
  other arithmetic: 14.6 us -> 2.39 us
  starting transfers between devices: 6.05 us -> 0 us
  local copies, waits for them, and re-layouts: 10.3 us -> 4.58 us
    pallas_call x0 -> x1, Pallas kernels: none -> 36.8 us  [mix_all(): pl.pallas_call(functools.partial(mixer_kernel, levels), out_shape=jax.Sha...]
    ppermute x5 -> x0, waiting for transfers between devices: 28.7 us -> none  [from_partner(): return lax.ppermute(block, axis, route)]
    dot_general x4 -> x0, matrix products: 10.6 us -> none  [the longest x1 6.24 us: block_terms(): jnp.einsum('lts,thl->hts', masks, weights_all[:, :, :inner], precision=HI...]
    ppermute x5 -> x0, starting transfers between devices: 6.05 us -> none  [from_partner(): return lax.ppermute(block, axis, route)]
    convert_element_type x5 -> x0, other arithmetic: 5.53 us -> none  [the longest x2 2.37 us: per_device(): carried = (carry_decay[:, None, None] * other_state).astype(jnp.bfloat16)]
    unnamed x3 -> x0, matrix products: 3.94 us -> none
    reduce_sum x1 -> x0, other arithmetic: 3.31 us -> none  [finish(): mean_square = jnp.mean(mixed * mixed, axis=-1, keepdims=True)]
    unnamed x28 -> x5, local copies, waits for them, and re-layouts: 5.51 us -> 4.5 us
  transfers between devices with their start and end apart: 5 -> 0, of which waited for: 2 -> 0; matrix products, arithmetic and copies ran while one was open for 16% -> 0% of each run, Pallas kernels for 55% -> 0%
where the time goes in v2:
time: 133 us
  Pallas kernels  126 us (95%)
  local copies, waits for them, and re-layouts  4.58 us (3%)
  other arithmetic  2.39 us (2%)
    pallas_call x1, Pallas kernels, project(): pl.pallas_call(gather_kernel, out_shape=(jax.ShapeDtypeStruct((length, na...  89.1 us
    pallas_call x1, Pallas kernels, mix_all(): pl.pallas_call(functools.partial(mixer_kernel, levels), out_shape=jax.Sha...  36.8 us
    unnamed x5, local copies, waits for them, and re-layouts  4.5 us

profile of v2, /device:TPU:0, one launch (start us, length us, event | category | flops | bytes accessed | tf_op | source)
XLA Modules:
  0.0 133.0 jit_solution(4608933900877056225)
XLA Ops:
  0.0 1.4 %copy.8 = bf16[1024,320]{1,0:T(8,128)(2,1)S(1)} copy(bf16[1024,320]{0,1:T(8,128)(2,1)} %param.11) | data formatting | bytes 1310720 | tf_op args[4]
  1.5 0.1 pad.3.clone
  1.5 2.4 %maximum_maximum_fusion.a_ref = bf16[1024,640]{1,0:T(8,128)(2,1)} fusion(bf16[1024,320]{1,0:T(8,128)(2,1)S(1)} %copy.8, bf16[1024,128]{1,0:T(8,128)(2,1)} %param.9, bf16[1024,128]{1,0:T(8,128)(2,1)} %param.8, bf16[640]{0:T(1024)(128)(2,1)S(1)} %pad.3.clone), kind=kLoop, calls=%fused_computation | loop fusion | flops 5242880 | bytes 2491648 | tf_op jit(solution)/shard_map/concatenate | solution.py:188
  3.9 0.0 copy-start
  3.9 89.1 %gather_project.1 = (bf16[256,256]{1,0:T(8,128)(2,1)}, f32[256,384]{1,0:T(8,128)}, bf16[256,2048]{1,0:T(8,128)(2,1)}) custom-call(bf16[256,4096]{1,0:T(8,128)(2,1)} %bitcast.5, bf16[1024,640]{1,0:T(8,128)(2,1)} %maximum_maximum_fusion.a_ref, bf16[1024,2048]{1,0:T(8,128)(2,1)} %v_ref.1), custom_call_target="tpu_custom_call" | custom-call | tf_op jit(solution)/shard_map/gather_project/pallas_call | solution.py:193
  93.0 0.0 copy-done
  93.1 0.8 copy.9
  93.8 36.8 %mixer.1 = bf16[256,2048]{1,0:T(8,128)(2,1)} custom-call(bf16[256,256]{1,0:T(8,128)(2,1)} %get-tuple-element.8.qk_ref, f32[256,384]{1,0:T(8,128)} %get-tuple-element.9.lam_ref, bf16[256,2048]{1,0:T(8,128)(2,1)} %get-tuple-element.10.val_ref, f32[256,16]{1,0:T(8,128)} %bitcast.6, f32[1,2048]{1,0:T(1,128)} %bitcast.7), custom_call_target="tpu_custom_call" | custom-call | tf_op jit(solution)/shard_map/mixer/pallas_call | solution.py:416
  130.7 2.3 %copy.11 = bf16[1,256,2048]{2,1,0:T(8,128)(2,1)} copy(bf16[1,256,2048]{2,1,0:T(8,128)(2,1)} %bitcast.4) | data formatting | bytes 2097152
  (1 shorter events, 0.0 us)
Async XLA Ops:
  3.9 89.1 %copy-start = (f32[1,256,16]{1,2,0:T(8,128)S(1)}, f32[1,256,16]{1,2,0:T(8,128)}, u32[]{:S(2)}) copy-start(f32[1,256,16]{1,2,0:T(8,128)} %param.12) | copy-start | bytes 49156

commit v3 on v2

--- a/solution.py
+++ b/solution.py
@@ -13,8 +13,9 @@
 VMEM_LIMIT = 63 * 1024 * 1024
 
 
-CHUNKS = 8
-SHARED = 2
+CHUNKS = 16
+SHARED = 5
+PACK = 4
 
 
 def gather_kernel(x_ref, a_ref, v_ref, qk_ref, lam_ref, val_ref, big_a, big_v, acc_a, acc_v,
@@ -109,11 +110,11 @@
 
     lax.fori_loop(0, wide // tile, first, 0)
 
-    def multiply(way, pair):
-        span = 2 * rows
-        at = pair + side * (CHUNKS // 2 - 1 - 2 * pair)
+    def multiply(way, pack):
+        span = PACK * rows
+        at = pack + side * (CHUNKS // PACK - 1 - 2 * pack)
         low = pl.multiple_of(at * span, span)
-        for i in (2 * pair, 2 * pair + 1):
+        for i in range(PACK * pack, PACK * (pack + 1)):
             for k, (own, big) in enumerate(pairs):
                 at_i = i + side * (CHUNKS - 1 - 2 * i)
                 other = pl.ds(pl.multiple_of(at_i * rows + (1 - core) * half, half), half)
@@ -141,16 +142,23 @@
             start(relay_copy(i))
         start(core_copy(way, i))
 
-    seen = set()
+    seen = {}
 
     def note(way, i):
         take(way, i)
-        seen.add((way, i))
-        if (way, i ^ 1) in seen:
-            ready.append((way, i // 2))
+        pack = (way, i // PACK)
+        seen[pack] = seen.get(pack, 0) + 1
+        if seen[pack] == PACK:
+            ready.append(pack)
 
     lag = 2
+    crossed = []
+    for step in range(SHARED + lag):
+        crossed += [(way, step) for way in range(2) if step < SHARED]
+        crossed += [(2, step - lag)] if step >= lag else []
+    taken = 0
     for step in range(direct + lag):
+        due, ready[:] = list(ready), []
         if step < direct:
             note(0, step)
             note(1, step)
@@ -158,17 +166,17 @@
                 start(own_copy(0, step + 2))
                 start(own_copy(1, step + 2))
         if step >= lag:
-            back = step - lag
-            if back < SHARED:
-                note(0, CHUNKS - 1 - back)
-                note(1, CHUNKS - 1 - back)
-            note(2, back)
-        if step < direct and len(ready) > 1:
-            multiply(*ready.pop(0))
-    while len(ready) > 1:
-        multiply(*ready.pop(0))
-    for back in range(SHARED):
-        note(2, CHUNKS - 1 - back)
+            note(2, step - lag)
+        while taken < min(len(crossed), (3 * step - 1) // 2):
+            way, i = crossed[taken]
+            note(way, CHUNKS - 1 - i)
+            taken += 1
+        for pack in due:
+            multiply(*pack)
+    while taken < len(crossed):
+        way, i = crossed[taken]
+        note(way, CHUNKS - 1 - i)
+        taken += 1
     while ready:
         multiply(*ready.pop(0))
     for copy in started:

time: 133 us -> 123 us (0.925)
  Pallas kernels: 126 us -> 116 us
    pallas_call x1, Pallas kernels: 89.1 us -> 79.9 us  [project(): pl.pallas_call(gather_kernel, out_shape=(jax.ShapeDtypeStruct((length, na...]
where the time goes in v3:
time: 123 us
  Pallas kernels  116 us (94%)
  local copies, waits for them, and re-layouts  4.58 us (4%)
  other arithmetic  2.39 us (2%)
    pallas_call x1, Pallas kernels, project(): pl.pallas_call(gather_kernel, out_shape=(jax.ShapeDtypeStruct((length, na...  79.9 us
    pallas_call x1, Pallas kernels, mix_all(): pl.pallas_call(functools.partial(mixer_kernel, levels), out_shape=jax.Sha...  36.3 us
    unnamed x5, local copies, waits for them, and re-layouts  4.5 us

profile of v3, /device:TPU:0, one launch (start us, length us, event | category | flops | bytes accessed | tf_op | source)
XLA Modules:
  0.0 123.2 jit_solution(17636781859386697708)
XLA Ops:
  0.0 1.4 %copy.8 = bf16[1024,320]{1,0:T(8,128)(2,1)S(1)} copy(bf16[1024,320]{0,1:T(8,128)(2,1)} %param.11) | data formatting | bytes 1310720 | tf_op args[4]
  1.5 0.1 pad.3.clone
  1.5 2.4 %maximum_maximum_fusion.a_ref = bf16[1024,640]{1,0:T(8,128)(2,1)} fusion(bf16[1024,320]{1,0:T(8,128)(2,1)S(1)} %copy.8, bf16[1024,128]{1,0:T(8,128)(2,1)} %param.9, bf16[1024,128]{1,0:T(8,128)(2,1)} %param.8, bf16[640]{0:T(1024)(128)(2,1)S(1)} %pad.3.clone), kind=kLoop, calls=%fused_computation | loop fusion | flops 5242880 | bytes 2491648 | tf_op jit(solution)/shard_map/concatenate | solution.py:196
  3.9 0.0 copy-start
  3.9 79.9 %gather_project.1 = (bf16[256,256]{1,0:T(8,128)(2,1)}, f32[256,384]{1,0:T(8,128)}, bf16[256,2048]{1,0:T(8,128)(2,1)}) custom-call(bf16[256,4096]{1,0:T(8,128)(2,1)} %bitcast.5, bf16[1024,640]{1,0:T(8,128)(2,1)} %maximum_maximum_fusion.a_ref, bf16[1024,2048]{1,0:T(8,128)(2,1)} %v_ref.1), custom_call_target="tpu_custom_call" | custom-call | tf_op jit(solution)/shard_map/gather_project/pallas_call | solution.py:201
  83.8 0.0 copy-done
  83.8 0.8 copy.9
  84.6 36.3 %mixer.1 = bf16[256,2048]{1,0:T(8,128)(2,1)} custom-call(bf16[256,256]{1,0:T(8,128)(2,1)} %get-tuple-element.8.qk_ref, f32[256,384]{1,0:T(8,128)} %get-tuple-element.9.lam_ref, bf16[256,2048]{1,0:T(8,128)(2,1)} %get-tuple-element.10.val_ref, f32[256,16]{1,0:T(8,128)} %bitcast.6, f32[1,2048]{1,0:T(1,128)} %bitcast.7), custom_call_target="tpu_custom_call" | custom-call | tf_op jit(solution)/shard_map/mixer/pallas_call | solution.py:424
  120.9 2.3 %copy.11 = bf16[1,256,2048]{2,1,0:T(8,128)(2,1)} copy(bf16[1,256,2048]{2,1,0:T(8,128)(2,1)} %bitcast.4) | data formatting | bytes 2097152
  (1 shorter events, 0.0 us)
Async XLA Ops:
  3.9 79.9 %copy-start = (f32[1,256,16]{1,2,0:T(8,128)S(1)}, f32[1,256,16]{1,2,0:T(8,128)}, u32[]{:S(2)}) copy-start(f32[1,256,16]{1,2,0:T(8,128)} %param.12) | copy-start | bytes 49156

commit v4 on v3

--- a/solution.py
+++ b/solution.py
@@ -19,7 +19,8 @@
 
 
 def gather_kernel(x_ref, a_ref, v_ref, qk_ref, lam_ref, val_ref, big_a, big_v, acc_a, acc_v,
-                  direct_sem, core_sem, send_sem, relay_sem, z_sem, fwd_sem):
+                  direct_sem, core_sem, send_sem, relay_sem, z_sem, fwd_sem,
+                  own_a, own_v, own_sem):
     depth = a_ref.shape[0]
     rows = depth // CHUNKS
     half = rows // 2
@@ -96,16 +97,22 @@
     for i in range(2):
         start(own_copy(0, i))
         start(own_copy(1, i))
+    local = [pltpu.make_async_copy(a_ref, own_a, own_sem.at[0]),
+             pltpu.make_async_copy(v_ref, own_v, own_sem.at[1])]
+    for copy in local:
+        copy.start()
+    for copy in local:
+        copy.wait()
 
     own_at = pl.ds(pl.multiple_of(owners[0] * depth, depth), depth)
     tile = 512
     wide = acc_v.shape[1]
-    acc_a[...] = jnp.dot(x_ref[:, own_at], a_ref[...], preferred_element_type=jnp.float32)
+    acc_a[...] = jnp.dot(x_ref[:, own_at], own_a[...], preferred_element_type=jnp.float32)
 
     def first(n, carry):
         cols = pl.ds(pl.multiple_of(n * tile, tile), tile)
         acc_v[:, cols] = jnp.dot(
-            x_ref[:, own_at], v_ref[:, cols], preferred_element_type=jnp.float32)
+            x_ref[:, own_at], own_v[:, cols], preferred_element_type=jnp.float32)
         return carry
 
     lax.fori_loop(0, wide // tile, first, 0)
@@ -205,7 +212,7 @@
             jax.ShapeDtypeStruct((length, lams + fill), jnp.float32),
             jax.ShapeDtypeStruct((length, wide), jnp.bfloat16),
         ),
-        in_specs=[vmem] * 3,
+        in_specs=[vmem] + [pl.BlockSpec(memory_space=pl.ANY)] * 2,
         out_specs=(vmem,) * 3,
         scratch_shapes=[
             pltpu.VMEM((3, depth, columns), jnp.bfloat16),
@@ -218,6 +225,9 @@
             dma((CHUNKS, 2)),
             dma((3, SHARED, 2)),
             dma((3, CHUNKS, 2)),
+            pltpu.VMEM((depth, columns), jnp.bfloat16),
+            pltpu.VMEM((depth, wide), jnp.bfloat16),
+            dma((2,)),
         ],
         compiler_params=pltpu.CompilerParams(
             collective_id=0, has_side_effects=True, vmem_limit_bytes=VMEM_LIMIT),

time: 123 us -> 122 us (level)
    pallas_call x1, Pallas kernels: 79.9 us -> 78.5 us  [project(): pl.pallas_call(gather_kernel, out_shape=(jax.ShapeDtypeStruct((length, na...]
where the time goes in v4:
time: 122 us
  Pallas kernels  115 us (94%)
  local copies, waits for them, and re-layouts  4.58 us (4%)
  other arithmetic  2.39 us (2%)
    pallas_call x1, Pallas kernels, project(): pl.pallas_call(gather_kernel, out_shape=(jax.ShapeDtypeStruct((length, na...  78.5 us
    pallas_call x1, Pallas kernels, mix_all(): pl.pallas_call(functools.partial(mixer_kernel, levels), out_shape=jax.Sha...  36.3 us
    unnamed x5, local copies, waits for them, and re-layouts  4.5 us

profile of v4, /device:TPU:0, one launch (start us, length us, event | category | flops | bytes accessed | tf_op | source)
XLA Modules:
  0.0 121.8 jit_solution(9897469205621557439)
XLA Ops:
  0.0 1.4 %copy.8 = bf16[1024,320]{1,0:T(8,128)(2,1)S(1)} copy(bf16[1024,320]{0,1:T(8,128)(2,1)} %param.11) | data formatting | bytes 1310720 | tf_op args[4]
  1.5 0.1 pad.3.clone
  1.5 2.4 %maximum_maximum_fusion.a_ref = bf16[1024,640]{1,0:T(8,128)(2,1)} fusion(bf16[1024,320]{1,0:T(8,128)(2,1)S(1)} %copy.8, bf16[1024,128]{1,0:T(8,128)(2,1)} %param.9, bf16[1024,128]{1,0:T(8,128)(2,1)} %param.8, bf16[640]{0:T(1024)(128)(2,1)S(1)} %pad.3.clone), kind=kLoop, calls=%fused_computation | loop fusion | flops 5242880 | bytes 2491648 | tf_op jit(solution)/shard_map/concatenate | solution.py:203
  3.9 0.0 copy-start
  3.9 78.5 %gather_project.1 = (bf16[256,256]{1,0:T(8,128)(2,1)}, f32[256,384]{1,0:T(8,128)}, bf16[256,2048]{1,0:T(8,128)(2,1)}) custom-call(bf16[256,4096]{1,0:T(8,128)(2,1)} %bitcast.5, bf16[1024,640]{1,0:T(8,128)(2,1)} %maximum_maximum_fusion.a_ref, bf16[1024,2048]{1,0:T(8,128)(2,1)} %v_ref.1), custom_call_target="tpu_custom_call" | custom-call | tf_op jit(solution)/shard_map/gather_project/pallas_call | solution.py:208
  82.4 0.0 copy-done
  82.4 0.8 copy.9
  83.2 36.3 %mixer.1 = bf16[256,2048]{1,0:T(8,128)(2,1)} custom-call(bf16[256,256]{1,0:T(8,128)(2,1)} %get-tuple-element.8.qk_ref, f32[256,384]{1,0:T(8,128)} %get-tuple-element.9.lam_ref, bf16[256,2048]{1,0:T(8,128)(2,1)} %get-tuple-element.10.val_ref, f32[256,16]{1,0:T(8,128)} %bitcast.6, f32[1,2048]{1,0:T(1,128)} %bitcast.7), custom_call_target="tpu_custom_call" | custom-call | tf_op jit(solution)/shard_map/mixer/pallas_call | solution.py:434
  119.5 2.3 %copy.11 = bf16[1,256,2048]{2,1,0:T(8,128)(2,1)} copy(bf16[1,256,2048]{2,1,0:T(8,128)(2,1)} %bitcast.4) | data formatting | bytes 2097152
  (1 shorter events, 0.0 us)
Async XLA Ops:
  3.9 78.5 %copy-start = (f32[1,256,16]{1,2,0:T(8,128)S(1)}, f32[1,256,16]{1,2,0:T(8,128)}, u32[]{:S(2)}) copy-start(f32[1,256,16]{1,2,0:T(8,128)} %param.12) | copy-start | bytes 49156
